TPU v7x, 256 devices: a whole 4x4x8 slice. The times are simulated.
256 devices in a mesh: row: 8 (over z), col: 16 (over x_hi, y, core), rep: 2 (over x_lo).
Axes of the slice: x: 4 (x_hi: 2, x_lo: 2; x = x_hi * 2 + x_lo), y: 4, z: 8, core: 2. Of those that a mesh axis runs over, the one named last changes fastest.
Arguments:
- descriptors: float32 [2048, 256], P('rep', 'col'), may hold values from -6 to 6
- landmarks: float32 [12288, 256], P('row', 'col'), may hold values from -6 to 6
- whitening: float32 [12288, 12288], P('row', 'col'), may hold values from -1 to 1
- assign: int32 [2048], replicated, may hold values from 0 to 4095
Outputs:
- cluster_sums: float32 [4096, 12288], P(('row', 'rep'), 'col')
All inputs are finite; a program needn't handle non-finite values.
Results may differ from a plain program's by a relative error of at most 0.00016.
Values sent between devices are 32-bit elements; how exact they have to be, the bound alone decides.
A program may use at most 64 MiB of HBM per device.

v0:
```python
import functools

import jax
import jax.numpy as jnp
from jax import lax
from jax.experimental import pallas as pl
from jax.experimental.pallas import tpu as pltpu
from jax.sharding import PartitionSpec as P

SPREAD = 51
CLUSTERS = 4096

f32, bf16 = jnp.float32, jnp.bfloat16
MESH = pl.DeviceIdType.MESH


def nn(a, b):
    return lax.dot_general(a, b, (((1,), (0,)), ((), ())), preferred_element_type=f32)


def nt(a, b):
    return lax.dot_general(a, b, (((1,), (1,)), ((), ())), preferred_element_type=f32)


def split(x):
    high = x.astype(bf16)
    return high, (x - high.astype(f32)).astype(bf16)


def ones_where(mask):
    return jnp.where(mask, 1.0, 0.0).astype(bf16)


def iota(shape, axis):
    return lax.broadcasted_iota(jnp.int32, shape, axis)


def kernel(slots, dense, points_ref, centres_ref, white_ref, assign_ref, out_ref, over_ref,
           lbuf, dbuf, wfull, wh, wl, dh, dl, lh, ll, pick, fold, pos, kh, kl, ah, al,
           sbuf, rbuf, local_sem, gs, gr, fs, fr, zs, zr):
    rows = assign_ref.shape[1]
    part = points_ref.shape[1]
    centres = centres_ref.shape[1]
    cols = white_ref.shape[1]
    owned = out_ref.shape[0]
    half = slots // 2
    z, c, p = lax.axis_index("row"), lax.axis_index("col"), lax.axis_index("rep")
    nz = lax.axis_size("row")
    xh, y, core = c // 8, lax.rem(c // 2, 4), lax.rem(c, 2)
    x = 2 * xh + p

    def device(dx, dy, other=0):
        to = lax.rem(x + dx + 4, 4)
        col = (to // 2) * 8 + lax.rem(y + dy + 4, 4) * 2 + (1 - core if other else core)
        return {"row": z, "col": col, "rep": lax.rem(to, 2)}

    sibling = device(0, 0, 1)
    ahead = {"row": lax.rem(z + 1, nz), "col": c, "rep": p}
    behind = {"row": lax.rem(z + nz - 1, nz), "col": c, "rep": p}

    def d_slot(dx, dy):
        at = lax.rem(x + dx + 4, 4)
        return dbuf.at[at // 2, lax.rem(at, 2), lax.rem(y + dy + 4, 4), core]

    def l_slot(flip, dy):
        return lbuf.at[1 - xh if flip else xh, lax.rem(y + dy + 4, 4), core]

    own_points = pltpu.make_async_copy(points_ref, d_slot(0, 0), local_sem.at[0])
    own_centres = pltpu.make_async_copy(centres_ref, l_slot(0, 0), local_sem.at[1])
    own_white = pltpu.make_async_copy(white_ref, wfull, local_sem.at[2])
    own_points.start()
    own_centres.start()
    own_white.start()

    barrier = pltpu.get_barrier_semaphore()
    near = [sibling, ahead, behind, device(1, 0), device(-1, 0), device(0, 1), device(0, -1)]
    for target in near:
        pl.semaphore_signal(barrier, inc=1, device_id=target, device_id_type=MESH)
    pl.semaphore_wait(barrier, len(near))

    own_points.wait()
    own_centres.wait()

    DIR = (1, -1)
    SIDE = (0, -1, 1, 2)
    ON = ((0, 3), (1, 2))

    def sender(index, ref, target):
        return pltpu.make_async_remote_copy(ref, ref, gs.at[index], gr.at[index], device_id=target, device_id_type=MESH)

    def halves(ref, w):
        return ref.at[:, pl.ds(w * (part // 2), part // 2)]

    moves = {}
    for w in range(2):
        d = DIR[w]
        moves["dy", w] = (w, d_slot(0, 0), device(0, d), d_slot(0, -d))
        moves["dyy", w] = (2 + w, halves(d_slot(0, -d), w), device(0, d), halves(d_slot(0, 2), w))
        for s in range(4):
            moves["dx", w, s] = (4 + w * 4 + s, d_slot(0, SIDE[s]), device(d, 0), d_slot(-d, SIDE[s]))
        for i, s in enumerate(ON[w]):
            moves["dxx", w, s] = (12 + w * 2 + i, d_slot(-d, SIDE[s]), device(d, 0), d_slot(2, SIDE[s]))
        for o in range(2):
            moves["ly", w, o] = (17 + w * 2 + o, l_slot(o, 0), device(0, d), l_slot(o, -d))
        moves["lyy", w] = (21 + w, l_slot(w, -d), device(0, d), l_slot(w, 2))
    moves["lx"] = (16, l_slot(0, 0), device(2 * p - 1, 0), l_slot(1, 0))

    def send(*key):
        index, ref, target, _ = moves[key if len(key) > 1 else key[0]]
        sender(index, ref, target).start()

    def arrive(*key):
        index, _, target, ref = moves[key if len(key) > 1 else key[0]]
        sender(index, ref, target).wait_recv()

    def hand(index, theirs):
        k = 1 - core if theirs else core
        if index < 4:
            ref = lbuf.at[:, lax.rem(y + SIDE[index] + 4, 4), k]
        else:
            at = lax.rem(x + SIDE[index - 4] + 4, 4)
            ref = dbuf.at[at // 2, lax.rem(at, 2), :, k]
        return pltpu.make_async_remote_copy(ref, ref, fs.at[index], fr.at[index], device_id=sibling, device_id_type=MESH)

    for w in range(2):
        send("dy", w)
        send("dx", w, 0)
    send("lx")
    for w in range(2):
        send("ly", w, 0)

    assign = assign_ref[...]
    owner_of = assign // owned

    def owner_at(j):
        far = nz // 2 - (j + 1) // 2
        step = jnp.where(lax.rem(j, 2) == 1, far, nz - far) if not isinstance(j, int) else (far if j % 2 else nz - far)
        return lax.rem(z + step, nz) * 2 + p

    def members(owner):
        return ones_where(iota((owned, rows), 0) == assign - owner * owned)

    if not dense:
        before = ones_where(iota((128, 128), 0) < iota((128, 128), 1))
        base = jnp.zeros((16, 1), f32)
        for block in range(rows // 128):
            at = pl.ds(block * 128, 128)
            mine = ones_where(iota((16, 128), 0) == owner_of[:, block * 128:(block + 1) * 128])
            mine32 = mine.astype(f32)
            pos[:, at] = jnp.sum(mine32 * (nn(mine, before) + base), axis=0, keepdims=True)
            base = base + jnp.sum(mine32, axis=1, keepdims=True)
        below = ones_where(iota((owned, owned), 0) < iota((owned, owned), 1))
        counts = nt(ones_where(iota((64, rows), 0) == assign // 64), ones_where(iota((64, rows), 0) == assign % 64))
        group = ones_where(iota((16, 64), 0) == iota((16, 64), 1) // (owned // 64))
        used = jnp.sum(nn(group, ones_where(counts > 0.5)), axis=1, keepdims=True)
        excess = jnp.maximum(used - slots, base - fold.shape[2])
        over_ref[...] = jnp.broadcast_to(jnp.max(excess, axis=0, keepdims=True), over_ref.shape)

    def prepare(j):
        owner = owner_at(j)
        take = fold.shape[2]
        rank = jnp.where(owner_of == owner, pos[...], -1.0).astype(jnp.int32)
        chosen = ones_where(iota((take, rows), 0) == rank)
        pick[j] = chosen
        belongs = members(owner)
        counts = nt(jnp.ones((8, rows), bf16), belongs)
        active = counts > 0.5
        order = nn(ones_where(active), below).astype(jnp.int32)
        squeeze = ones_where((iota((slots, owned), 0) == order[0:1]) & active[0:1])
        fold[j] = nn(squeeze, nt(belongs, chosen).astype(bf16)).astype(bf16)

    def halve_white():
        own_white.wait()

        @pl.loop(0, centres // 128)
        def _(i):
            at = pl.ds(pl.multiple_of(i * 128, 128), 128)
            high, low = split(wfull[at, :])
            wh[at, :] = high
            wl[at, :] = low

    def prepare_at(j):
        if not dense:
            pl.loop(j, j + 1)(prepare)

    def halve_centres(i):
        hand(i, True).wait_recv()
        at = lax.rem(y + SIDE[i] + 4, 4)
        total = jnp.zeros((1, centres), f32)
        for k in range(2):
            centre = lbuf[k, at]
            total = total + jnp.sum((centre * centre).reshape(32, centres), axis=0, keepdims=True)
            lh[k, at], ll[k, at] = split(centre)
        return total

    def halve_points(i):
        hand(4 + i, True).wait_recv()
        at = lax.rem(x + SIDE[i] + 4, 4)
        hi, r = at // 2, lax.rem(at, 2)
        for k in range(4):
            dh[hi, r, k], dl[hi, r, k] = split(dbuf[hi, r, k])

    halve_white()
    for w in range(2):
        arrive("dy", w)
        send("dyy", w)
        send("dx", 0, 1 + w)
        send("dx", 1, 1 + w)
    arrive("lx")
    for w in range(2):
        send("ly", w, 1)
    hand(0, False).start()
    prepare_at(0)
    for w in range(2):
        arrive("dyy", w)
    for w in range(2):
        send("dx", w, 3)
    hand(4, False).start()
    for w in range(2):
        arrive("ly", w, 0)
    send("lyy", 0)
    for w in range(2):
        arrive("dx", w, 0)
    send("dxx", 0, 0)
    prepare_at(1)
    for s in (1, 2):
        for w in range(2):
            arrive("dx", w, s)
        send("dxx", 1, s)
    for w in range(2):
        arrive("ly", w, 1)
    send("lyy", 1)
    hand(1, False).start()
    hand(2, False).start()
    squares = halve_centres(0)
    for w in range(2):
        arrive("dx", w, 3)
    send("dxx", 0, 3)
    hand(5, False).start()
    hand(6, False).start()
    prepare_at(2)
    halve_points(0)
    squares = squares + halve_centres(1)
    squares = squares + halve_centres(2)
    for w in range(2):
        arrive("lyy", w)
    hand(3, False).start()
    halve_points(1)
    halve_points(2)
    for w in range(2):
        for s in ON[w]:
            arrive("dxx", w, s)
    hand(7, False).start()
    squares = squares + halve_centres(3)
    halve_points(3)

    def flat(ref, lanes=slice(None)):
        value = ref[:, :, :, :, lanes]
        return value.reshape(value.shape[0] * value.shape[1] * value.shape[2] * value.shape[3], value.shape[4])

    def points_of(r, ref, lanes=slice(None)):
        value = ref[:, r, :, :, :, lanes]
        return value.reshape(value.shape[0] * value.shape[1] * value.shape[2] * value.shape[3], value.shape[4])

    def picked_points(picked, ref):
        return nt(picked[:, :part], points_of(0, ref)) + nt(picked[:, part:], points_of(1, ref))

    def kernel_rows(xhi, xlo, at):
        x = xhi + xlo
        norm = jnp.sum(x * x, axis=1, keepdims=True)
        xhi, xlo = xhi.astype(bf16), xlo.astype(bf16)
        for i in range(centres // 512):
            on = slice(i * 512, (i + 1) * 512)
            inner = nn(xhi, flat(lh, on)) + nn(xhi, flat(ll, on)) + nn(xlo, flat(lh, on))
            value = jnp.exp((norm + squares[:, on] - 2.0 * inner) * (-1.0 / (2.0 * SPREAD)))
            kh[at, on], kl[at, on] = split(value)

    if dense:
        eye = ones_where(iota((256, 256), 0) == iota((256, 256), 1))

        for r in range(2):
            @pl.loop(0, part // 256)
            def _(i):
                at = pl.ds(pl.multiple_of(i * 256, 256), 256)
                to = pl.ds(pl.multiple_of(r * part + i * 256, 256), 256)
                kernel_rows(nt(eye, points_of(r, dh, at)), nt(eye, points_of(r, dl, at)), to)

    def sum_rows(j, i):
        if dense:
            chosen, on = members(owner_at(j)), slice(0, rows)
        else:
            take = fold.shape[2]
            picked, on = pick[j], slice(i * take, (i + 1) * take)
            kernel_rows(picked_points(picked, dh), picked_points(picked, dl), on)
            chosen = fold[j]
        at = pl.ds(i * slots, slots)

        def lane_tile(lanes):
            ah[at, lanes], al[at, lanes] = split(nn(chosen, kh[on, lanes]) + nn(chosen, kl[on, lanes]))

        if dense:
            @pl.loop(0, centres // 512)
            def _(k):
                lane_tile(pl.ds(pl.multiple_of(k * 512, 512), 512))
        else:
            for k in range(centres // 512):
                lane_tile(slice(k * 512, (k + 1) * 512))

    def blocks(first, count):
        if dense and count > 1:
            @pl.loop(0, count)
            def _(i):
                sum_rows(first + i, i)
        else:
            for i in range(count):
                sum_rows(first + i, i)
        every = slice(0, count * slots)
        return nn(ah[every, :], wh[...]) + nn(ah[every, :], wl[...]) + nn(al[every, :], wh[...])

    def hop(way, step, part_of):
        at = pl.ds(part_of * half, half)
        return pltpu.make_async_remote_copy(sbuf.at[way, step, at], rbuf.at[way, step, at],
                                            zs.at[way, step, part_of], zr.at[way, step, part_of],
                                            device_id=(ahead, behind)[way], device_id_type=MESH)

    made = blocks(0, 1)
    sbuf[0, 0, :half] = made[:half]
    sbuf[1, 0, half:] = made[half:]
    hop(0, 0, 0).start()
    hop(1, 0, 1).start()

    @pl.loop(1, 4)
    def _(step):
        made = blocks(2 * step - 1, 2)
        sbuf[0, step] = made[:slots]
        sbuf[1, step] = made[slots:]
        for turn in range(2):
            for way in range(2):
                part_of = 1 - way if turn == 0 else way
                at = pl.ds(part_of * half, half)

                def join():
                    hop(way, step - 1, part_of).wait_recv()
                    sbuf[way, step, at] += rbuf[way, step - 1, at]

                if turn == 1:
                    join()
                else:
                    pl.when(step > 1)(join)
                hop(way, step, part_of).start()
        if not dense:
            prepare(2 * step + 1)
            pl.when(step < 3)(lambda: prepare(2 * step + 2))

    made = blocks(7, 1)
    if not dense:
        belongs = members(lax.rem(z, nz) * 2 + p)
        counts = nn(belongs, jnp.ones((rows, slots), bf16))
        order = nn(ones_where(iota((owned, owned), 0) > iota((owned, owned), 1)), ones_where(counts > 0.5))
        spread = ones_where((order.astype(jnp.int32) == iota((owned, slots), 1)) & (counts > 0.5))
    for way in range(2):
        for part_of in range(2):
            hop(way, 3, part_of).wait_recv()
    total = made + rbuf[0, 3] + rbuf[1, 3]
    if dense:
        out_ref[...] = total
        over_ref[...] = jnp.zeros_like(over_ref)
    else:
        high, low = split(total)
        rest = (total - high.astype(f32) - low.astype(f32)).astype(bf16)
        out_ref[...] = nn(spread, high) + nn(spread, low) + nn(spread, rest)

    for index, ref, target, _ in moves.values():
        sender(index, ref, target).wait_send()
    for i in range(8):
        hand(i, False).wait_send()
    for way in range(2):
        for step in range(4):
            for part_of in range(2):
                if step > 0 or part_of == way:
                    hop(way, step, part_of).wait_send()


def call(slots, take, dense, points, centres, white, assign):
    part = points.shape[1]
    count, cols = white.shape
    rows = assign.shape[1]
    owned = CLUSTERS // (lax.axis_size("row") * lax.axis_size("rep"))
    held = rows if dense else 2 * take
    dma = pltpu.SemaphoreType.DMA
    small = dense
    return pl.pallas_call(
        functools.partial(kernel, slots, dense),
        out_shape=[jax.ShapeDtypeStruct((owned, cols), f32), jax.ShapeDtypeStruct((8, 128), f32)],
        in_specs=[pl.BlockSpec(memory_space=pl.ANY)] * 3 + [pl.BlockSpec(memory_space=pltpu.VMEM)],
        out_specs=[pl.BlockSpec(memory_space=pltpu.VMEM)] * 2,
        scratch_shapes=[
            pltpu.VMEM((2, 4, 2, 16, count), f32),
            pltpu.VMEM((2, 2, 4, 2, 16, part), f32),
            pltpu.VMEM((count, cols), f32),
            pltpu.VMEM((count, cols), bf16),
            pltpu.VMEM((count, cols), bf16),
            pltpu.VMEM((2, 2, 4, 2, 16, part), bf16),
            pltpu.VMEM((2, 2, 4, 2, 16, part), bf16),
            pltpu.VMEM((2, 4, 2, 16, count), bf16),
            pltpu.VMEM((2, 4, 2, 16, count), bf16),
            pltpu.VMEM((8, 16, 128) if small else (8, take, rows), bf16),
            pltpu.VMEM((8, 16, 128) if small else (8, slots, take), bf16),
            pltpu.VMEM((1, rows), f32),
            pltpu.VMEM((held, count), bf16),
            pltpu.VMEM((held, count), bf16),
            pltpu.VMEM((2 * slots, count), bf16),
            pltpu.VMEM((2 * slots, count), bf16),
            pltpu.VMEM((2, 4, slots, cols), f32),
            pltpu.VMEM((2, 4, slots, cols), f32),
            dma((3,)), dma((23,)), dma((23,)), dma((8,)), dma((8,)),
            dma((2, 4, 2)), dma((2, 4, 2)),
        ],
        compiler_params=pltpu.CompilerParams(
            collective_id=1 if dense else 0, has_side_effects=True, vmem_limit_bytes=60 * 2**20),
    )(points, centres, white, assign)


def per_device(descriptors, landmarks, whitening, assign):
    owned = CLUSTERS // (lax.axis_size("row") * lax.axis_size("rep"))
    args = descriptors.T, landmarks.T, whitening, assign.reshape(1, -1)
    sums, over = call(owned // 2, 256, False, *args)
    return lax.cond(over[0, 0] > 0.5, lambda: call(owned, 256, True, *args)[0], lambda: sums)


def solution(mesh):
    placed = (P("rep", "col"), P("row", "col"), P("row", "col"), P())
    return jax.shard_map(
        per_device, mesh=mesh, in_specs=placed, out_specs=P(("row", "rep"), "col"), check_vma=False
    )
```

profile of v0, /device:TPU:1, one launch (start us, length us, event | category | flops | bytes accessed | tf_op | source)
XLA Modules:
  0.0 70.8 jit_solution(15107663823257124128)
XLA Ops:
  0.0 0.0 copy-start.2
  0.0 0.0 copy-start
  0.0 0.0 copy-start.1
  0.0 68.0 %shard_map.48 = (f32[256,768]{1,0:T(8,128)S(1)}, f32[8,128]{1,0:T(8,128)}) custom-call(f32[16,1024]{1,0:T(8,128)} %bitcast.6, f32[16,1536]{1,0:T(8,128)} %bitcast.4, f32[1536,768]{1,0:T(8,128)} %white_ref.1, s32[1,2048]{1,0:T(1,128)} %bitcast.8), custom_call_target="tpu_custom_call" | custom-call | tf_op jit(solution)/shard_map/pallas_call | solution.py:392
  68.1 1.2 %slice.3 = f32[1,1]{1,0:T(1,128)} slice(f32[8,128]{1,0:T(8,128)} %get-tuple-element.24), slice={[0:1], [0:1]} | slice | bytes 8 | tf_op jit(solution)/shard_map/slice | solution.py:428
  69.9 0.0 copy-done.2
  69.9 0.0 copy-done
  69.9 0.0 copy-done.1
  69.9 0.9 %copy.10 = f32[256,768]{1,0:T(8,128)} copy(f32[256,768]{1,0:T(8,128)S(1)} %get-tuple-element.26) | data formatting | bytes 1572864
  (1 shorter events, 0.0 us)
Async XLA Ops:
  0.0 69.9 %copy-start.2 = (s32[2048]{0:T(1024)S(1)}, s32[2048]{0:T(1024)}, u32[]{:S(2)}) copy-start(s32[2048]{0:T(1024)} %param.9) | copy-start | bytes 24580
  0.0 69.9 %copy-start = (f32[1536,16]{0,1:T(8,128)S(1)}, f32[1536,16]{0,1:T(8,128)}, u32[]{:S(2)}) copy-start(f32[1536,16]{0,1:T(8,128)} %param.7) | copy-start | bytes 294916
  0.0 69.9 %copy-start.1 = (f32[1024,16]{0,1:T(8,128)S(1)}, f32[1024,16]{0,1:T(8,128)}, u32[]{:S(2)}) copy-start(f32[1024,16]{0,1:T(8,128)} %param.6) | copy-start | bytes 196612
where the time goes:
time: 71 us; the launch traced here: 70.8 us
  Pallas kernels  68 us (96%)
  local copies, waits for them, and re-layouts  2.09 us (3%)
    pallas_call x1, Pallas kernels, call(): pl.pallas_call(functools.partial(kernel, slots, dense), out_shape=[jax.Sh...  68 us

commit v1 on v0

--- a/solution.py
+++ b/solution.py
@@ -73,7 +73,7 @@
     own_white.start()
 
     barrier = pltpu.get_barrier_semaphore()
-    near = [sibling, ahead, behind, device(1, 0), device(-1, 0), device(0, 1), device(0, -1)]
+    near = [sibling, ahead, behind, device(1, 0), device(-1, 0), device(0, 1), device(0, -1), device(0, 2)]
     for target in near:
         pl.semaphore_signal(barrier, inc=1, device_id=target, device_id_type=MESH)
     pl.semaphore_wait(barrier, len(near))
@@ -88,14 +88,10 @@
     def sender(index, ref, target):
         return pltpu.make_async_remote_copy(ref, ref, gs.at[index], gr.at[index], device_id=target, device_id_type=MESH)
 
-    def halves(ref, w):
-        return ref.at[:, pl.ds(w * (part // 2), part // 2)]
-
     moves = {}
     for w in range(2):
         d = DIR[w]
         moves["dy", w] = (w, d_slot(0, 0), device(0, d), d_slot(0, -d))
-        moves["dyy", w] = (2 + w, halves(d_slot(0, -d), w), device(0, d), halves(d_slot(0, 2), w))
         for s in range(4):
             moves["dx", w, s] = (4 + w * 4 + s, d_slot(0, SIDE[s]), device(d, 0), d_slot(-d, SIDE[s]))
         for i, s in enumerate(ON[w]):
@@ -103,6 +99,7 @@
         for o in range(2):
             moves["ly", w, o] = (17 + w * 2 + o, l_slot(o, 0), device(0, d), l_slot(o, -d))
         moves["lyy", w] = (21 + w, l_slot(w, -d), device(0, d), l_slot(w, 2))
+    moves["dyy"] = (2, d_slot(0, 0), device(0, 2), d_slot(0, 2))
     moves["lx"] = (16, l_slot(0, 0), device(2 * p - 1, 0), l_slot(1, 0))
 
     def send(*key):
@@ -125,6 +122,7 @@
     for w in range(2):
         send("dy", w)
         send("dx", w, 0)
+    send("dyy")
     send("lx")
     for w in range(2):
         send("ly", w, 0)
@@ -154,7 +152,7 @@
         group = ones_where(iota((16, 64), 0) == iota((16, 64), 1) // (owned // 64))
         used = jnp.sum(nn(group, ones_where(counts > 0.5)), axis=1, keepdims=True)
         excess = jnp.maximum(used - slots, base - fold.shape[2])
-        over_ref[...] = jnp.broadcast_to(jnp.max(excess, axis=0, keepdims=True), over_ref.shape)
+        over_ref[0, 0] = jnp.max(excess)
 
     def prepare(j):
         owner = owner_at(j)
@@ -203,19 +201,17 @@
     halve_white()
     for w in range(2):
         arrive("dy", w)
-        send("dyy", w)
         send("dx", 0, 1 + w)
         send("dx", 1, 1 + w)
+    arrive("dyy")
+    for w in range(2):
+        send("dx", w, 3)
+    hand(4, False).start()
     arrive("lx")
     for w in range(2):
         send("ly", w, 1)
     hand(0, False).start()
     prepare_at(0)
-    for w in range(2):
-        arrive("dyy", w)
-    for w in range(2):
-        send("dx", w, 3)
-    hand(4, False).start()
     for w in range(2):
         arrive("ly", w, 0)
     send("lyy", 0)
@@ -364,7 +360,7 @@
     total = made + rbuf[0, 3] + rbuf[1, 3]
     if dense:
         out_ref[...] = total
-        over_ref[...] = jnp.zeros_like(over_ref)
+        over_ref[0, 0] = jnp.float32(0.0)
     else:
         high, low = split(total)
         rest = (total - high.astype(f32) - low.astype(f32)).astype(bf16)
@@ -391,9 +387,9 @@
     small = dense
     return pl.pallas_call(
         functools.partial(kernel, slots, dense),
-        out_shape=[jax.ShapeDtypeStruct((owned, cols), f32), jax.ShapeDtypeStruct((8, 128), f32)],
+        out_shape=[jax.ShapeDtypeStruct((owned, cols), f32), jax.ShapeDtypeStruct((1, 1), f32)],
         in_specs=[pl.BlockSpec(memory_space=pl.ANY)] * 3 + [pl.BlockSpec(memory_space=pltpu.VMEM)],
-        out_specs=[pl.BlockSpec(memory_space=pltpu.VMEM)] * 2,
+        out_specs=[pl.BlockSpec(memory_space=pltpu.VMEM), pl.BlockSpec(memory_space=pltpu.SMEM)],
         scratch_shapes=[
             pltpu.VMEM((2, 4, 2, 16, count), f32),
             pltpu.VMEM((2, 2, 4, 2, 16, part), f32),

time: 71 us -> 69.6 us (0.980)
  local copies, waits for them, and re-layouts: 2.09 us -> 0.89 us
    slice x1 -> x0, local copies, waits for them, and re-layouts: 1.19 us -> none  [per_device(): over[0, 0] > 0.5]
where the time goes in v1:
time: 69.6 us; the launch traced here: 69.5 us
  Pallas kernels  67.9 us (98%)
  local copies, waits for them, and re-layouts  0.89 us (1%)
  between operations  0.74 us (1%)
    pallas_call x1, Pallas kernels, call(): pl.pallas_call(functools.partial(kernel, slots, dense), out_shape=[jax.Sh...  67.9 us

profile of v1, /device:TPU:1, one launch (start us, length us, event | category | flops | bytes accessed | tf_op | source)
XLA Modules:
  0.0 69.5 jit_solution(598213402344549910)
XLA Ops:
  0.0 0.0 copy-start.2
  0.0 0.0 copy-start
  0.0 0.0 copy-start.1
  0.0 67.9 %shard_map.48 = (f32[256,768]{1,0:T(8,128)S(1)}, f32[1,1]{1,0:T(1,128)}) custom-call(f32[16,1024]{1,0:T(8,128)} %bitcast.6, f32[16,1536]{1,0:T(8,128)} %bitcast.4, f32[1536,768]{1,0:T(8,128)} %white_ref.1, s32[1,2048]{1,0:T(1,128)} %bitcast.8), custom_call_target="tpu_custom_call" | custom-call | tf_op jit(solution)/shard_map/pallas_call | solution.py:388
  68.6 0.0 copy-done.2
  68.6 0.0 copy-done
  68.6 0.0 copy-done.1
  68.6 0.9 %copy.10 = f32[256,768]{1,0:T(8,128)} copy(f32[256,768]{1,0:T(8,128)S(1)} %get-tuple-element.26) | data formatting | bytes 1572864
  (1 shorter events, 0.0 us)
Async XLA Ops:
  0.0 68.6 %copy-start.2 = (s32[2048]{0:T(1024)S(1)}, s32[2048]{0:T(1024)}, u32[]{:S(2)}) copy-start(s32[2048]{0:T(1024)} %param.9) | copy-start | bytes 24580
  0.0 68.6 %copy-start = (f32[1536,16]{0,1:T(8,128)S(1)}, f32[1536,16]{0,1:T(8,128)}, u32[]{:S(2)}) copy-start(f32[1536,16]{0,1:T(8,128)} %param.7) | copy-start | bytes 294916
  0.0 68.6 %copy-start.1 = (f32[1024,16]{0,1:T(8,128)S(1)}, f32[1024,16]{0,1:T(8,128)}, u32[]{:S(2)}) copy-start(f32[1024,16]{0,1:T(8,128)} %param.6) | copy-start | bytes 196612

commit v2 on v1

--- a/solution.py
+++ b/solution.py
@@ -218,7 +218,6 @@
     for w in range(2):
         arrive("dx", w, 0)
     send("dxx", 0, 0)
-    prepare_at(1)
     for s in (1, 2):
         for w in range(2):
             arrive("dx", w, s)
@@ -234,13 +233,14 @@
     send("dxx", 0, 3)
     hand(5, False).start()
     hand(6, False).start()
-    prepare_at(2)
+    prepare_at(1)
     halve_points(0)
     squares = squares + halve_centres(1)
     squares = squares + halve_centres(2)
     for w in range(2):
         arrive("lyy", w)
     hand(3, False).start()
+    prepare_at(2)
     halve_points(1)
     halve_points(2)
     for w in range(2):

time: 69.6 us -> 69.8 us (level)
  no operation moved by 1% of the time
where the time goes in v2:
time: 69.8 us; the launch traced here: 69.7 us
  Pallas kernels  68 us (97%)
  local copies, waits for them, and re-layouts  0.89 us (1%)
  between operations  0.74 us (1%)
    pallas_call x1, Pallas kernels, call(): pl.pallas_call(functools.partial(kernel, slots, dense), out_shape=[jax.Sh...  68 us

profile of v2, /device:TPU:1, one launch (start us, length us, event | category | flops | bytes accessed | tf_op | source)
XLA Modules:
  0.0 69.7 jit_solution(7296986062275854695)
XLA Ops:
  0.0 0.0 copy-start.2
  0.0 0.0 copy-start
  0.0 0.0 copy-start.1
  0.0 68.0 %shard_map.48 = (f32[256,768]{1,0:T(8,128)S(1)}, f32[1,1]{1,0:T(1,128)}) custom-call(f32[16,1024]{1,0:T(8,128)} %bitcast.6, f32[16,1536]{1,0:T(8,128)} %bitcast.4, f32[1536,768]{1,0:T(8,128)} %white_ref.1, s32[1,2048]{1,0:T(1,128)} %bitcast.8), custom_call_target="tpu_custom_call" | custom-call | tf_op jit(solution)/shard_map/pallas_call | solution.py:388
  68.8 0.0 copy-done.2
  68.8 0.0 copy-done
  68.8 0.0 copy-done.1
  68.8 0.9 %copy.10 = f32[256,768]{1,0:T(8,128)} copy(f32[256,768]{1,0:T(8,128)S(1)} %get-tuple-element.26) | data formatting | bytes 1572864
  (1 shorter events, 0.0 us)
Async XLA Ops:
  0.0 68.8 %copy-start.2 = (s32[2048]{0:T(1024)S(1)}, s32[2048]{0:T(1024)}, u32[]{:S(2)}) copy-start(s32[2048]{0:T(1024)} %param.9) | copy-start | bytes 24580
  0.0 68.8 %copy-start = (f32[1536,16]{0,1:T(8,128)S(1)}, f32[1536,16]{0,1:T(8,128)}, u32[]{:S(2)}) copy-start(f32[1536,16]{0,1:T(8,128)} %param.7) | copy-start | bytes 294916
  0.0 68.8 %copy-start.1 = (f32[1024,16]{0,1:T(8,128)S(1)}, f32[1024,16]{0,1:T(8,128)}, u32[]{:S(2)}) copy-start(f32[1024,16]{0,1:T(8,128)} %param.6) | copy-start | bytes 196612
